TPU v7x, 128 devices: a whole 4x4x4 slice. The times are simulated.
128 devices in a mesh: dp: 16 (over y, z_lo, core), mp: 8 (over z_hi, x).
Axes of the slice: x: 4, y: 4, z: 4 (z_hi: 2, z_lo: 2; z = z_hi * 2 + z_lo), core: 2. Of those that a mesh axis runs over, the one named last changes fastest.
Arguments:
- doc_ids: int32 [16, 512], P('dp'), may hold values from 0 to 128255
- doc_lengths: int32 [16], P('dp'), may hold values from 128 to 512
- activations: bfloat16 [8192, 4096], P('dp'), may hold values from -6 to 6
- out_grads: bfloat16 [8192, 14336], P('dp'), may hold values from -0.29882812 to 0.29882812
- input_basis: bfloat16 [4096, 2048], P(None, 'mp'), may hold values from -0.09375 to 0.09375
- output_basis: bfloat16 [14336, 7168], P('dp', 'mp'), may hold values from -0.046875 to 0.046875
- eigenvalues: bfloat16 [2048, 7168], P(None, 'mp'), may hold values from 0.5 to 50
- query_left: bfloat16 [64, 32, 2048], P('dp'), may hold values from -0.125 to 0.125
- query_right: bfloat16 [64, 32, 7168], P('dp', None, 'mp'), may hold values from -0.0625 to 0.0625
Outputs:
- scores: float32 [16, 64], P('dp')
Inputs may be any that keep to these rules, and one draw needn't show every extreme that they name: `doc_lengths`: the live tokens are the first ones of each document.
All inputs are finite; a program needn't handle non-finite values.
Results may differ from a plain program's by a relative error of at most 0.023.
Values may be sent and summed in bfloat16 or wider, within the bound.
No kernel may reach another device: no remote copies, remote signals or barrier semaphores. Data moves between devices by JAX's collectives and lax.ppermute only.
A program may use at most 192 MiB of HBM per device.

v0:
```python
import jax
import jax.numpy as jnp
from jax import lax
from jax.sharding import PartitionSpec as P

damping = 0.5


def laid_out(blocks, dim):
    blocks = jnp.moveaxis(blocks, 0, dim)
    dims = blocks.shape
    return blocks.reshape(*dims[:dim], dims[dim] * dims[dim + 1], *dims[dim + 2 :])


def from_everyone(array, axis):
    length = lax.axis_size(axis)
    return lax.all_to_all(
        jnp.broadcast_to(array[None], (length, *array.shape)), axis, 0, 0, tiled=True
    )


def gather_directly(array, axis, dim):
    return laid_out(from_everyone(array, axis), dim)


def taken_together(array, axis):
    everything = from_everyone(array, axis)
    return jnp.sum(everything, axis=0)


def token_weights(doc_ids, doc_lengths):
    positions = jnp.arange(doc_ids.shape[1], dtype=jnp.int32)
    active = positions[None, :] < doc_lengths[:, None]
    matches = (doc_ids[:, :, None] == doc_ids[:, None, :]) & active[:, None, :]
    repeats = jnp.sum(matches.astype(jnp.float32), axis=2)
    return jnp.where(active, 1.0 / jnp.maximum(repeats, 1.0), 0.0)


def per_device(
    doc_ids,
    doc_lengths,
    activations,
    out_grads,
    input_basis,
    output_basis,
    eigenvalues,
    query_left,
    query_right,
):
    tok_rows = activations.shape[0]
    shard_rows = output_basis.shape[0]
    out_cols = output_basis.shape[1]
    rotated_share = jnp.dot(activations, input_basis, preferred_element_type=jnp.float32).astype(
        jnp.bfloat16
    )
    rotated_in = gather_directly(rotated_share, "mp", 1)
    empty = jnp.zeros((tok_rows, out_cols), jnp.float32)
    running = empty
    pieces = lax.all_gather(output_basis, "dp", axis=0, tiled=True)
    for member in range(pieces.shape[0] // shard_rows):
        grad_cols = lax.dynamic_slice_in_dim(out_grads, member * shard_rows, shard_rows, 1)
        partial_value = jnp.dot(
            grad_cols,
            pieces[member * shard_rows : (member + 1) * shard_rows],
            preferred_element_type=jnp.float32,
        )
        running = running + lax.optimization_barrier(partial_value.astype(jnp.bfloat16)).astype(
            jnp.float32
        )
    rotated_out = running.astype(jnp.bfloat16)
    weights = token_weights(doc_ids, doc_lengths)
    docs_here = doc_ids.shape[0]
    acts_doc = rotated_in.reshape(docs_here, -1, rotated_in.shape[1])
    grads_doc = rotated_out.reshape(docs_here, -1, out_cols)
    scaled = (weights[:, :, None] * grads_doc.astype(jnp.float32)).astype(jnp.bfloat16)
    gradient = jnp.einsum("dti,dtj->dij", acts_doc, scaled, preferred_element_type=jnp.float32)
    conditioned = (gradient / (eigenvalues.astype(jnp.float32) + damping)).astype(jnp.bfloat16)
    rank_rows = query_left.shape[1]
    left_part = lax.all_gather(query_left, "dp", axis=0, tiled=True)
    right_part = lax.all_gather(query_right, "dp", axis=0, tiled=True)
    number = left_part.shape[0]
    left_rows = left_part.reshape(number * rank_rows, left_part.shape[2])
    right_rows = right_part.reshape(number * rank_rows, right_part.shape[2]).astype(jnp.float32)
    mixture = jnp.einsum("ri,dij->drj", left_rows, conditioned, preferred_element_type=jnp.float32)
    values = jnp.sum((mixture * right_rows[None]).reshape(docs_here, number, -1), axis=2)
    return taken_together(values, "mp")


def solution(mesh):
    return jax.shard_map(
        per_device,
        mesh=mesh,
        in_specs=(
            P("dp", None),
            P("dp"),
            P("dp", None),
            P("dp", None),
            P(None, "mp"),
            P("dp", "mp"),
            P(None, "mp"),
            P("dp", None, None),
            P("dp", None, "mp"),
        ),
        out_specs=P("dp", None),
        check_vma=False,
    )
```

profile of v0, /device:TPU:0, one launch (start us, length us, event | category | flops | bytes accessed | tf_op | source)
XLA Modules:
  0.0 307.4 jit_solution(3509372564559330316)
XLA Ops:
  6.5 0.0 copy-start
  6.5 0.0 all-gather.8.cloned.1.call-start
  6.5 0.7 all-gather.8.cloned.1.call-update
  7.3 0.0 all-gather.4.cloned.1.call-start
  7.3 0.7 all-gather.4.cloned.1.call-update
  8.0 0.0 all-gather.6.cloned.1.call-start
  8.1 0.7 all-gather.6.cloned.1.call-update
  8.7 0.0 copy-done
  8.8 3.4 %convolution_convert_fusion = bf16[512,256]{1,0:T(8,128)(2,1)S(1)} fusion(bf16[512,4096]{1,0:T(8,128)(2,1)} %param.11, bf16[4096,256]{1,0:T(8,128)(2,1)S(1)} %copy-done), kind=kOutput, calls=%fused_computation.56 | convolution fusion | flops 1073872896 | bytes 6553600 | tf_op jit(solution)/shard_map/dot_general | solution.py:53
  12.2 0.1 copy.17
  12.3 1.5 broadcast_in_dim.7
  13.8 0.0 copy-start.2
  13.8 7.8 %all-to-all-start = ((bf16[8,512,256]{1,2,0:T(8,128)(2,1)}), bf16[8,512,256]{1,2,0:T(8,128)(2,1)}, u32[]{:S(2)}, u32[]{:S(2)}) async-start(bf16[8,512,256]{1,2,0:T(8,128)(2,1)} %broadcast_in_dim.7), calls=%async_computation | async-start | bytes 4194304 | tf_op jit(solution)/shard_map/all_to_all | solution.py:17
  22.3 0.0 copy-done.2
  22.3 0.3 convert_reduce_fusion
  22.7 46.0 %all-gather.8.cloned.1.call-done = bf16[64,32,896]{2,1,0:T(8,128)(2,1)} async-done(((bf16[4,32,896]{2,1,0:T(8,128)(2,1)}), bf16[64,32,896]{2,1,0:T(8,128)(2,1)}) %all-gather.8.cloned.1.call-update) | async-done | bytes 3670032 | tf_op jit(solution)/shard_map/all_gather | solution.py:80
  68.6 5.5 %bitcast_convert_fusion = f32[1,2048,896]{2,1,0:T(8,128)} fusion(bf16[1,2048,896]{2,1,0:T(8,128)(2,1)} %bitcast.24), kind=kLoop, calls=%fused_computation.3 | loop fusion | flops 1835008 | bytes 11010048 | tf_op jit(solution)/shard_map/convert_element_type | solution.py:83
  74.1 8.7 %copy.18 = f32[1,2048,896]{1,2,0:T(8,128)} copy(f32[1,2048,896]{2,1,0:T(8,128)} %bitcast_convert_fusion) | data formatting | bytes 14680064 | tf_op jit(solution)/shard_map/convert_element_type | solution.py:83
  82.8 121.5 %all-gather.4.cloned.1.call-done = bf16[14336,896]{1,0:T(8,128)(2,1)} async-done(((bf16[896,896]{1,0:T(8,128)(2,1)}), bf16[14336,896]{1,0:T(8,128)(2,1)}) %all-gather.4.cloned.1.call-update) | async-done | bytes 25690128 | tf_op jit(solution)/shard_map/all_gather | solution.py:59
  204.3 0.0 copy-start.3
  204.3 3.1 fusion.36
  207.4 4.6 %fusion.39 = bf16[512,896]{1,0:T(8,128)(2,1)} fusion(bf16[14336,896]{1,0:T(8,128)(2,1)} %all-gather.4.cloned.1.call-done, bf16[512,14336]{1,0:T(8,128)(2,1)} %param.12), kind=kOutput, calls=%fused_computation.41 | convolution fusion | flops 822542336 | bytes 3440640 | tf_op jit(solution)/shard_map/dot_general | solution.py:62
  212.0 4.6 %fusion.42 = bf16[512,896]{1,0:T(8,128)(2,1)} fusion(bf16[14336,896]{1,0:T(8,128)(2,1)} %all-gather.4.cloned.1.call-done, bf16[512,14336]{1,0:T(8,128)(2,1)} %param.12), kind=kOutput, calls=%fused_computation.42 | convolution fusion | flops 822542336 | bytes 3440640 | tf_op jit(solution)/shard_map/dot_general | solution.py:62
  216.6 3.8 %fusion.45 = bf16[512,896]{1,0:T(8,128)(2,1)} fusion(bf16[14336,896]{1,0:T(8,128)(2,1)} %all-gather.4.cloned.1.call-done, bf16[512,14336]{1,0:T(8,128)(2,1)} %param.12), kind=kOutput, calls=%fused_computation.43 | convolution fusion | flops 822542336 | bytes 3440640 | tf_op jit(solution)/shard_map/dot_general | solution.py:62
  220.5 3.9 %fusion.48 = bf16[512,896]{1,0:T(8,128)(2,1)} fusion(bf16[14336,896]{1,0:T(8,128)(2,1)} %all-gather.4.cloned.1.call-done, bf16[512,14336]{1,0:T(8,128)(2,1)} %param.12), kind=kOutput, calls=%fused_computation.44 | convolution fusion | flops 822542336 | bytes 3440640 | tf_op jit(solution)/shard_map/dot_general | solution.py:62
  224.4 0.0 copy-done.3
  224.4 3.4 %fusion.51 = bf16[512,896]{1,0:T(8,128)(2,1)} fusion(bf16[14336,896]{1,0:T(8,128)(2,1)S(1)} %copy-done.3, bf16[512,14336]{1,0:T(8,128)(2,1)} %param.12), kind=kOutput, calls=%fused_computation.45 | convolution fusion | flops 822542336 | bytes 3440640 | tf_op jit(solution)/shard_map/dot_general | solution.py:62
  227.7 3.3 %fusion.54 = bf16[512,896]{1,0:T(8,128)(2,1)} fusion(bf16[14336,896]{1,0:T(8,128)(2,1)S(1)} %copy-done.3, bf16[512,14336]{1,0:T(8,128)(2,1)} %param.12), kind=kOutput, calls=%fused_computation.46 | convolution fusion | flops 822542336 | bytes 3440640 | tf_op jit(solution)/shard_map/dot_general | solution.py:62
  231.1 3.4 %fusion.57 = bf16[512,896]{1,0:T(8,128)(2,1)} fusion(bf16[14336,896]{1,0:T(8,128)(2,1)S(1)} %copy-done.3, bf16[512,14336]{1,0:T(8,128)(2,1)} %param.12), kind=kOutput, calls=%fused_computation.47 | convolution fusion | flops 822542336 | bytes 3440640 | tf_op jit(solution)/shard_map/dot_general | solution.py:62
  234.4 3.4 %fusion.60 = bf16[512,896]{1,0:T(8,128)(2,1)} fusion(bf16[14336,896]{1,0:T(8,128)(2,1)S(1)} %copy-done.3, bf16[512,14336]{1,0:T(8,128)(2,1)} %param.12), kind=kOutput, calls=%fused_computation.48 | convolution fusion | flops 822542336 | bytes 3440640 | tf_op jit(solution)/shard_map/dot_general | solution.py:62
  237.8 3.3 %fusion.63 = bf16[512,896]{1,0:T(8,128)(2,1)} fusion(bf16[14336,896]{1,0:T(8,128)(2,1)S(1)} %copy-done.3, bf16[512,14336]{1,0:T(8,128)(2,1)} %param.12), kind=kOutput, calls=%fused_computation.49 | convolution fusion | flops 822542336 | bytes 3440640 | tf_op jit(solution)/shard_map/dot_general | solution.py:62
  241.1 3.4 %fusion.66 = bf16[512,896]{1,0:T(8,128)(2,1)} fusion(bf16[14336,896]{1,0:T(8,128)(2,1)S(1)} %copy-done.3, bf16[512,14336]{1,0:T(8,128)(2,1)} %param.12), kind=kOutput, calls=%fused_computation.50 | convolution fusion | flops 822542336 | bytes 3440640 | tf_op jit(solution)/shard_map/dot_general | solution.py:62
  244.5 3.3 %fusion.69 = bf16[512,896]{1,0:T(8,128)(2,1)} fusion(bf16[14336,896]{1,0:T(8,128)(2,1)S(1)} %copy-done.3, bf16[512,14336]{1,0:T(8,128)(2,1)} %param.12), kind=kOutput, calls=%fused_computation.51 | convolution fusion | flops 822542336 | bytes 3440640 | tf_op jit(solution)/shard_map/dot_general | solution.py:62
  247.8 3.3 %fusion.72 = bf16[512,896]{1,0:T(8,128)(2,1)} fusion(bf16[14336,896]{1,0:T(8,128)(2,1)S(1)} %copy-done.3, bf16[512,14336]{1,0:T(8,128)(2,1)} %param.12), kind=kOutput, calls=%fused_computation.52 | convolution fusion | flops 822542336 | bytes 3440640 | tf_op jit(solution)/shard_map/dot_general | solution.py:62
  251.1 3.6 %fusion.75 = bf16[512,896]{1,0:T(8,128)(2,1)} fusion(bf16[14336,896]{1,0:T(8,128)(2,1)S(1)} %copy-done.3, bf16[512,14336]{1,0:T(8,128)(2,1)} %param.12), kind=kOutput, calls=%fused_computation.53 | convolution fusion | flops 822542336 | bytes 3440640 | tf_op jit(solution)/shard_map/dot_general | solution.py:62
  254.7 3.3 %fusion.78 = bf16[512,896]{1,0:T(8,128)(2,1)} fusion(bf16[14336,896]{1,0:T(8,128)(2,1)S(1)} %copy-done.3, bf16[512,14336]{1,0:T(8,128)(2,1)} %param.12), kind=kOutput, calls=%fused_computation.54 | convolution fusion | flops 822542336 | bytes 3440640 | tf_op jit(solution)/shard_map/dot_general | solution.py:62
  258.1 3.3 %fusion.81 = bf16[512,896]{1,0:T(8,128)(2,1)} fusion(bf16[14336,896]{1,0:T(8,128)(2,1)S(1)} %copy-done.3, bf16[512,14336]{1,0:T(8,128)(2,1)} %param.12), kind=kOutput, calls=%fused_computation.55 | convolution fusion | flops 822542336 | bytes 3440640 | tf_op jit(solution)/shard_map/dot_general | solution.py:62
  261.4 0.0 all-to-all-done
  261.4 0.0 all-gather.6.cloned.1.call-done
  261.4 0.0 copy-start.1
  261.4 24.7 %fusion = f32[2048]{0:T(1024)S(1)} fusion(f32[1,2048,896]{1,2,0:T(8,128)} %copy.18, bf16[2048,2048]{1,0:T(8,128)(2,1)} %bitcast.27, bf16[2048,896]{1,0:T(8,128)(2,1)} %param.15, bf16[512,2048]{0,1:T(8,128)(2,1)} %bitcast.1, f32[512]{0:T(512)S(1)} %divide_select_fusion, bf16[512,896]{1,0:T(8,128)(2,1)} %fusion.81, bf16[512,896]{1,0:T(8,128)(2,1)} %fusion.78, ...), kind=kOutput, calls=%fused_computation.1 | convolution fusion | flops 9422305280 | bytes 36186112 | tf_op jit(solution)/shard_map/ri,dij->drj/dot_general | solution.py:84
  286.1 0.1 reduce_sum.38
  286.1 0.1 reduce_sum.39
  286.3 14.0 %all_to_all.10 = f32[8,1,64]{2,1,0:T(1,128)S(1)} all-to-all(f32[8,1,64]{2,1,0:T(1,128)S(1)} %broadcast_in_dim.9), channel_id=1, replica_groups=mesh['dp'=16,'mp'=8] {'mp'}, dimensions={0} | all-to-all | bytes 4096 | tf_op jit(solution)/shard_map/all_to_all | solution.py:17
  300.3 0.5 reduce_sum.40
  300.8 0.0 copy-done.1
  (3 shorter events, 0.0 us)
Async XLA Ops:
  6.5 2.2 copy-start
  6.5 62.1 %all-gather.8.cloned.1.call-start = ((), (), s32[]{:S(2)}) async-start(), calls=%async_computation.4 | async-start | bytes 3899392 | tf_op jit(solution)/shard_map/all_gather | solution.py:80
  7.3 197.1 %all-gather.4.cloned.1.call-start = ((), (), s32[]{:S(2)}) async-start(), calls=%async_computation.2 | async-start | bytes 27295744 | tf_op jit(solution)/shard_map/all_gather | solution.py:59
  8.0 253.4 %all-gather.6.cloned.1.call-start = ((), (), s32[]{:S(2)}) async-start(), calls=%async_computation.3 | async-start | bytes 8912896 | tf_op jit(solution)/shard_map/all_gather | solution.py:79
  13.8 8.5 %copy-start.2 = (s32[1,512]{1,0:T(1,128)S(1)}, s32[1,512]{1,0:T(1,128)}, u32[]{:S(2)}) copy-start(s32[1,512]{1,0:T(1,128)} %param.9) | copy-start | bytes 6148
  13.8 247.6 %all-to-all-start = ((bf16[8,512,256]{1,2,0:T(8,128)(2,1)}), bf16[8,512,256]{1,2,0:T(8,128)(2,1)}, u32[]{:S(2)}, u32[]{:S(2)}) async-start(bf16[8,512,256]{1,2,0:T(8,128)(2,1)} %broadcast_in_dim.7), calls=%async_computation | async-start | bytes 4194304 | tf_op jit(solution)/shard_map/all_to_all | solution.py:17
  204.3 20.0 %copy-start.3 = (bf16[14336,896]{1,0:T(8,128)(2,1)S(1)}, bf16[14336,896]{1,0:T(8,128)(2,1)}, u32[]{:S(2)}) copy-start(bf16[14336,896]{1,0:T(8,128)(2,1)} %all-gather.4.cloned.1.call-done) | copy-start | bytes 77070336
  261.4 39.4 %copy-start.1 = (bf16[4096,256]{1,0:T(8,128)(2,1)S(1)}, bf16[4096,256]{1,0:T(8,128)(2,1)}, u32[]{:S(2)}) copy-start(bf16[4096,256]{1,0:T(8,128)(2,1)} %param.13) | copy-start | bytes 6291460
Sparse Core Ops, SparseCore 0:
  9.1 59.5 all-gather.7
  70.3 133.9 all-gather.3
  206.0 52.8 all-gather.5
where the time goes:
time: 308 us; the launch traced here: 307 us
  waiting for transfers between devices  170 us (55%)
  matrix products  85.1 us (28%)
  blocking collectives  14 us (5%)
  between operations  13.8 us (4%)
  local copies, waits for them, and re-layouts  10.4 us (3%)
  starting transfers between devices  7.9 us (3%)
  other arithmetic  6.48 us (2%)
    all_gather x1, waiting for transfers between devices, per_device(): pieces = lax.all_gather(output_basis, 'dp', axis=0, tiled=True)  122 us
    dot_general x16, matrix products, per_device(): jnp.dot(grad_cols, pieces[member * shard_rows:(member + 1) * shard_rows],...  57.1 us
    all_gather x1, waiting for transfers between devices, per_device(): right_part = lax.all_gather(query_right, 'dp', axis=0, tiled=True)  46 us
    dot_general x1, matrix products, per_device(): jnp.einsum('ri,dij->drj', left_rows, conditioned, preferred_element_type=...  24.7 us
    all_to_all x1, blocking collectives, from_everyone(): lax.all_to_all(jnp.broadcast_to(array[None], (length, *array.shape)), axi...  14 us
    convert_element_type x1, local copies, waits for them, and re-layouts, per_device(): right_part.reshape(number * rank_rows, right_part.shape[2])  8.68 us
    all_to_all x1, starting transfers between devices, from_everyone(): lax.all_to_all(jnp.broadcast_to(array[None], (length, *array.shape)), axi...  7.83 us
  transfers between devices with their start and end apart: 4, of which 2 were waited for; matrix products, arithmetic and copies ran while one was open for 25% of the time, Pallas kernels for 0%

commit v1 on v0

--- a/solution.py
+++ b/solution.py
@@ -56,7 +56,10 @@
     rotated_in = gather_directly(rotated_share, "mp", 1)
     empty = jnp.zeros((tok_rows, out_cols), jnp.float32)
     running = empty
-    pieces = lax.all_gather(output_basis, "dp", axis=0, tiled=True)
+    devices = lax.axis_size("dp")
+    parts = jnp.stack([output_basis for _ in range(devices)])
+    parts = lax.all_to_all(parts, "dp", split_axis=0, concat_axis=0)
+    pieces = jnp.concatenate(parts, axis=0)
     for member in range(pieces.shape[0] // shard_rows):
         grad_cols = lax.dynamic_slice_in_dim(out_grads, member * shard_rows, shard_rows, 1)
         partial_value = jnp.dot(

time: 308 us -> 603 us (1.96)
  waiting for transfers between devices: 170 us -> 442 us
  local copies, waits for them, and re-layouts: 10.4 us -> 20.6 us
  starting transfers between devices: 7.9 us -> 17.5 us
    all_gather x1, waiting for transfers between devices: 46 us -> 286 us  [per_device(): right_part = lax.all_gather(query_right, 'dp', axis=0, tiled=True)]
    all_to_all x0 -> x1, waiting for transfers between devices: none -> 155 us  [per_device(): parts = lax.all_to_all(parts, 'dp', split_axis=0, concat_axis=0)]
    all_gather x1 -> x0, waiting for transfers between devices: 122 us -> none  [per_device(): pieces = lax.all_gather(output_basis, 'dp', axis=0, tiled=True)]
    another operation x0 -> x1, local copies, waits for them, and re-layouts: none -> 10.1 us  [per_device(): parts = jnp.stack([output_basis for _ in range(devices)])]
    all_to_all x0 -> x1, starting transfers between devices: none -> 6.06 us  [per_device(): parts = lax.all_to_all(parts, 'dp', split_axis=0, concat_axis=0)]
  transfers between devices with their start and end apart: 4 -> 4, of which waited for: 2 -> 2; matrix products, arithmetic and copies ran while one was open for 25% -> 13% of each run, Pallas kernels for 0% -> 0%
where the time goes in v1:
time: 603 us
  waiting for transfers between devices  442 us (73%)
  matrix products  86.8 us (14%)
  local copies, waits for them, and re-layouts  20.6 us (3%)
  starting transfers between devices  17.5 us (3%)
  blocking collectives  14.7 us (2%)
  between operations  14.2 us (2%)
  other arithmetic  6.43 us (1%)
    all_gather x1, waiting for transfers between devices, per_device(): right_part = lax.all_gather(query_right, 'dp', axis=0, tiled=True)  286 us
    all_to_all x1, waiting for transfers between devices, per_device(): parts = lax.all_to_all(parts, 'dp', split_axis=0, concat_axis=0)  155 us
    dot_general x16, matrix products, per_device(): jnp.dot(grad_cols, pieces[member * shard_rows:(member + 1) * shard_rows],...  58.7 us
    dot_general x1, matrix products, per_device(): jnp.einsum('ri,dij->drj', left_rows, conditioned, preferred_element_type=...  24.6 us
    all_to_all x1, blocking collectives, from_everyone(): lax.all_to_all(jnp.broadcast_to(array[None], (length, *array.shape)), axi...  14.7 us
  transfers between devices with their start and end apart: 4, of which 2 were waited for; matrix products, arithmetic and copies ran while one was open for 13% of the time, Pallas kernels for 0%

profile of v1, /device:TPU:0, one launch (start us, length us, event | category | flops | bytes accessed | tf_op | source)
XLA Modules:
  0.0 602.5 jit_solution(15030049772710823454)
XLA Ops:
  6.5 0.0 copy-start
  6.5 10.1 %stack.2 = bf16[16,896,896]{2,1,0:T(8,128)(2,1)} broadcast(bf16[896,896]{1,0:T(8,128)(2,1)} %param.14), dimensions={1,2} | broadcast | bytes 27295744 | tf_op jit(solution)/shard_map/stack | solution.py:60
  16.7 6.1 %all-to-all-start.1 = ((bf16[16,896,896]{2,1,0:T(8,128)(2,1)}), bf16[16,896,896]{2,1,0:T(8,128)(2,1)}, u32[]{:S(2)}, u32[]{:S(2)}) async-start(bf16[16,896,896]{2,1,0:T(8,128)(2,1)} %stack.2), calls=%async_computation.1 | async-start | bytes 51380224 | tf_op jit(solution)/shard_map/all_to_all | solution.py:61
  22.7 0.0 all-gather.5.cloned.1.call-start
  22.8 0.7 all-gather.5.cloned.1.call-update
  23.5 0.0 all-gather.3.cloned.1.call-start
  23.5 0.7 all-gather.3.cloned.1.call-update
  24.9 0.0 copy-done
  24.9 0.0 copy-start.2
  24.9 3.4 convolution_convert_fusion
  28.3 0.1 copy.17
  28.5 0.0 copy-done.2
  28.5 0.3 convert_reduce_fusion
  28.8 285.6 %all-gather.5.cloned.1.call-done = bf16[64,32,896]{2,1,0:T(8,128)(2,1)} async-done(((bf16[4,32,896]{2,1,0:T(8,128)(2,1)}), bf16[64,32,896]{2,1,0:T(8,128)(2,1)}) %all-gather.5.cloned.1.call-update) | async-done | bytes 3670032 | tf_op jit(solution)/shard_map/all_gather | solution.py:83
  314.4 5.5 bitcast_convert_fusion
  319.9 8.7 %copy.18 = f32[1,2048,896]{1,2,0:T(8,128)} copy(f32[1,2048,896]{2,1,0:T(8,128)} %bitcast_convert_fusion) | data formatting | bytes 14680064 | tf_op jit(solution)/shard_map/convert_element_type | solution.py:86
  328.6 155.4 %all-to-all-done.1 = bf16[16,896,896]{2,1,0:T(8,128)(2,1)} async-done(((bf16[16,896,896]{2,1,0:T(8,128)(2,1)}), bf16[16,896,896]{2,1,0:T(8,128)(2,1)}, u32[]{:S(2)}, u32[]{:S(2)}) %all-to-all-start.1) | async-done | bytes 25690144 | tf_op jit(solution)/shard_map/all_to_all | solution.py:61
  484.0 1.6 broadcast_in_dim.7
  485.5 11.4 %all-to-all-start = ((bf16[8,512,256]{1,2,0:T(8,128)(2,1)}), bf16[8,512,256]{1,2,0:T(8,128)(2,1)}, u32[]{:S(2)}, u32[]{:S(2)}) async-start(bf16[8,512,256]{1,2,0:T(8,128)(2,1)} %broadcast_in_dim.7), calls=%async_computation | async-start | bytes 4194304 | tf_op jit(solution)/shard_map/all_to_all | solution.py:17
  496.9 0.0 slice-start
  496.9 3.1 fusion.20
  500.0 0.0 slice-start.1
  500.0 4.0 fusion.21
  504.0 3.8 fusion.22
  507.9 4.0 fusion.23
  511.9 4.0 fusion.24
  515.9 3.8 fusion.25
  519.7 0.0 slice-done
  519.7 0.0 slice-done.1
  519.7 0.0 slice-done.2
  519.7 0.0 slice-done.3
  519.7 3.6 fusion.26
  523.3 3.6 fusion.27
  526.9 3.6 fusion.28
  530.5 3.5 fusion.29
  534.0 3.6 fusion.30
  537.6 3.6 fusion.31
  541.2 3.8 fusion.32
  544.9 3.6 fusion.33
  548.5 3.6 fusion.34
  552.1 3.6 fusion.35
  555.7 0.0 all-to-all-done
  555.7 24.6 %fusion = f32[2048]{0:T(1024)S(1)} fusion(f32[1,2048,896]{1,2,0:T(8,128)} %copy.18, bf16[2048,2048]{1,0:T(8,128)(2,1)} %bitcast.109, bf16[2048,896]{1,0:T(8,128)(2,1)} %param.15, bf16[512,2048]{0,1:T(8,128)(2,1)} %bitcast.1, f32[512]{0:T(512)S(1)} %divide_select_fusion, bf16[512,896]{1,0:T(8,128)(2,1)} %fusion.35, bf16[512,896]{1,0:T(8,128)(2,1)} %fusion.34, ...), kind=kOutput, calls=%fused_computation.1 | convolution fusion | flops 9422305280 | bytes 36186112 | tf_op jit(solution)/shard_map/ri,dij->drj/dot_general | solution.py:87
  580.3 0.1 reduce_sum.38
  580.4 0.1 reduce_sum.39
  580.5 14.7 %all_to_all.15 = f32[8,1,64]{2,1,0:T(1,128)S(1)} all-to-all(f32[8,1,64]{2,1,0:T(1,128)S(1)} %broadcast_in_dim.9), channel_id=1, replica_groups=mesh['dp'=16,'mp'=8] {'mp'}, dimensions={0} | all-to-all | bytes 4096 | tf_op jit(solution)/shard_map/all_to_all | solution.py:17
  595.2 0.5 reduce_sum.40
  595.7 0.0 copy-done.1
  (8 shorter events, 0.0 us)
Async XLA Ops:
  6.5 18.3 %copy-start = (bf16[4096,256]{1,0:T(8,128)(2,1)S(1)}, bf16[4096,256]{1,0:T(8,128)(2,1)}, u32[]{:S(2)}) copy-start(bf16[4096,256]{1,0:T(8,128)(2,1)} %param.13) | copy-start | bytes 6291460
  16.7 467.3 %all-to-all-start.1 = ((bf16[16,896,896]{2,1,0:T(8,128)(2,1)}), bf16[16,896,896]{2,1,0:T(8,128)(2,1)}, u32[]{:S(2)}, u32[]{:S(2)}) async-start(bf16[16,896,896]{2,1,0:T(8,128)(2,1)} %stack.2), calls=%async_computation.1 | async-start | bytes 51380224 | tf_op jit(solution)/shard_map/all_to_all | solution.py:61
  22.7 291.7 %all-gather.5.cloned.1.call-start = ((), (), s32[]{:S(2)}) async-start(), calls=%async_computation.4 | async-start | bytes 3899392 | tf_op jit(solution)/shard_map/all_gather | solution.py:83
  23.5 532.2 %all-gather.3.cloned.1.call-start = ((), (), s32[]{:S(2)}) async-start(), calls=%async_computation.3 | async-start | bytes 8912896 | tf_op jit(solution)/shard_map/all_gather | solution.py:82
  24.9 3.6 copy-start.2
  485.5 70.1 %all-to-all-start = ((bf16[8,512,256]{1,2,0:T(8,128)(2,1)}), bf16[8,512,256]{1,2,0:T(8,128)(2,1)}, u32[]{:S(2)}, u32[]{:S(2)}) async-start(bf16[8,512,256]{1,2,0:T(8,128)(2,1)} %broadcast_in_dim.7), calls=%async_computation | async-start | bytes 4194304 | tf_op jit(solution)/shard_map/all_to_all | solution.py:17
  496.9 22.8 %slice-start = ((s8[14680064]{0:T(1024)(128)(4,1)}), s8[4194304]{0:T(1024)(128)(4,1)S(1)}, s32[]{:S(2)}) async-start(s8[14680064]{0:T(1024)(128)(4,1)} %bitcast.107), calls=%async_computation.5 | async-start | bytes 8388608
  500.0 19.7 %slice-start.1 = ((s8[14680064]{0:T(1024)(128)(4,1)}), s8[4194304]{0:T(1024)(128)(4,1)S(1)}, s32[]{:S(2)}) async-start(s8[14680064]{0:T(1024)(128)(4,1)} %bitcast.107), calls=%async_computation.6 | async-start | bytes 8388608
  507.9 11.8 %slice-start.2 = ((s8[14680064]{0:T(1024)(128)(4,1)}), s8[4194304]{0:T(1024)(128)(4,1)S(1)}, s32[]{:S(2)}) async-start(s8[14680064]{0:T(1024)(128)(4,1)} %bitcast.107), calls=%async_computation.7 | async-start | bytes 8388608
  511.9 7.8 %slice-start.3 = ((s8[14680064]{0:T(1024)(128)(4,1)}), s8[2097152]{0:T(1024)(128)(4,1)S(1)}, s32[]{:S(2)}) async-start(s8[14680064]{0:T(1024)(128)(4,1)} %bitcast.107), calls=%async_computation.8 | async-start | bytes 4194304
  555.7 40.0 %copy-start.1 = (bf16[4096,256]{1,0:T(8,128)(2,1)S(1)}, bf16[4096,256]{1,0:T(8,128)(2,1)}, u32[]{:S(2)}) copy-start(bf16[4096,256]{1,0:T(8,128)(2,1)} %param.13) | copy-start | bytes 6291460
Sparse Core Ops, SparseCore 0:
  25.3 289.1 all-gather.4
  316.1 116.3 all-gather.2
